TPU v7x, 512 devices: a whole 4x8x8 slice. The times are simulated.
512 devices in a mesh: row: 32 (over y_hi, z), col: 16 (over x, y_lo, core).
Axes of the slice: x: 4, y: 8 (y_hi: 4, y_lo: 2; y = y_hi * 2 + y_lo), z: 8, core: 2. Of those that a mesh axis runs over, the one named last changes fastest.
Arguments:
- anc_inverse: bfloat16 [1, 32, 256, 2, 16, 256], P(None, 'row', None, None, 'col'), may hold values from -6 to 6
- factor_one: bfloat16 [1, 32, 256, 2, 16, 256], P(None, 'row', None, None, 'col'), may hold values from -0.0625 to 0.0625
- factor_two: bfloat16 [1, 32, 256, 1, 16, 256], P(None, 'row', None, None, 'col'), may hold values from -0.0625 to 0.0625
- parent_block: bfloat16 [1, 16, 256, 256], P(None, 'col'), may hold values from -0.375 to 0.375
- diag_one: float32 [2, 16, 256, 256], P(None, 'col'), may hold values from -6 to 6
- diag_two: float32 [1, 16, 256, 256], P(None, 'col'), may hold values from -6 to 6
- pattern_one: int32 [1, 32, 2, 16], P(None, 'row', None, 'col'), may hold values from 0 to 1
- pattern_two: int32 [1, 32, 1, 16], P(None, 'row', None, 'col'), may hold values from 0 to 1, as said below
- parent: int32 [1, 16], P(None, 'col'), may hold values from 0 to 31, as said below
Outputs:
- inv_one: bfloat16 [1, 32, 256, 2, 16, 256], P(None, 'row', None, None, 'col')
- diag_inv_one: float32 [2, 16, 256, 256], P(None, 'col')
- inv_two: bfloat16 [1, 32, 256, 1, 16, 256], P(None, 'row', None, None, 'col')
- parent_inv: bfloat16 [1, 16, 256, 256], P(None, 'col')
- diag_inv_two: float32 [1, 16, 256, 256], P(None, 'col')
Inputs may be any that keep to these rules, and one draw needn't show every extreme that they name: pattern_two[J, K] is zero wherever pattern_one[J, P(K)] is zero. parent[k, c] is a level-one supernode whose index leaves remainder c when divided by 16.
All inputs are finite; a program needn't handle non-finite values.
Results may differ from a plain program's by a relative error of at most 0.007.
Values may be sent and summed in bfloat16 or wider, within the bound.
A program may use at most 64 MiB of HBM per device.

v0:
```python
import jax
import jax.numpy as jnp
from jax import lax
from jax.sharding import PartitionSpec as P


def rows_step(whole_anc, anc_rows, block):

    def add_rows(total, piece, start):
        count = piece.shape[1]
        left = whole_anc.reshape(anc_rows * block, anc_rows * count * block)
        right = piece.reshape(anc_rows * count * block, piece.shape[3] * block)
        return jnp.dot(left, right, preferred_element_type=jnp.float32)

    return add_rows


def body(
    anc_inverse,
    factor_one,
    factor_two,
    parent_block,
    diag_one,
    diag_two,
    pattern_one,
    pattern_two,
    parent,
):
    anc_rows = anc_inverse.shape[0]
    block = anc_inverse.shape[2]
    first_count = factor_one.shape[3]
    second_count = factor_two.shape[3]
    grid_rows = lax.axis_size("row")
    grid_cols = lax.axis_size("col")
    first_factor = factor_one * pattern_one.astype(jnp.bfloat16)[:, :, None, :, :, None]
    second_factor = factor_two * pattern_two.astype(jnp.bfloat16)[:, :, None, :, :, None]
    first_empty = jnp.zeros((anc_rows * block, first_count * block), jnp.float32)
    second_empty = jnp.zeros((anc_rows * block, second_count * block), jnp.float32)
    whole_anc = lax.all_gather(anc_inverse, "col", axis=4, tiled=True).reshape(
        anc_rows * block, anc_rows, grid_rows, block
    )
    add_rows = rows_step(whole_anc, anc_rows, block)
    first_total = add_rows(
        first_empty, lax.all_gather(first_factor, "row", axis=1, tiled=True), jnp.int32(0)
    )
    first_shape = (anc_rows, block, first_count, block)
    second_shape = (anc_rows, block, second_count, block)
    first_keep = pattern_one.astype(jnp.float32)
    second_keep = pattern_two.astype(jnp.float32)
    first_inv = (-first_total.reshape(first_shape) * first_keep).astype(jnp.bfloat16)
    first_cols = first_factor.reshape(first_shape)
    second_cols = second_factor.reshape(second_shape)
    diag_part = jnp.einsum(
        "ixky,ixkz->kyz", first_cols, first_inv, preferred_element_type=jnp.float32
    )
    local_parent = parent.reshape(second_count) // grid_cols
    parent_cols = jnp.take(first_inv, local_parent, axis=2)
    cross_part = jnp.einsum(
        "ixky,ixkz->kyz", parent_cols, second_cols, preferred_element_type=jnp.float32
    )
    diag_sum, cross_sum = lax.psum((diag_part, cross_part), "row")
    first_diag = diag_one.reshape(first_count, block, block) - diag_sum
    parent_diag = jnp.take(first_diag.astype(jnp.bfloat16), local_parent, axis=0)
    coupling = parent_block.reshape(second_count, block, block)
    parent_inv = (
        -(
            jnp.einsum("kyx,kxz->kyz", parent_diag, coupling, preferred_element_type=jnp.float32)
            + cross_sum
        )
    ).astype(jnp.bfloat16)
    second_total = add_rows(
        second_empty, lax.all_gather(second_factor, "row", axis=1, tiled=True), jnp.int32(0)
    )
    side = jnp.einsum("ixky,kyz->ixkz", parent_cols, coupling, preferred_element_type=jnp.float32)
    second_inv = (-(second_total.reshape(second_shape) + side) * second_keep).astype(jnp.bfloat16)
    child_part = jnp.einsum(
        "ixky,ixkz->kyz", second_cols, second_inv, preferred_element_type=jnp.float32
    )
    child_sum = lax.psum(child_part.astype(jnp.bfloat16), "row").astype(jnp.float32)
    parent_terms = jnp.einsum(
        "kxy,kxz->kyz", coupling, parent_inv, preferred_element_type=jnp.float32
    )
    second_diag = diag_two.reshape(second_count, block, block) - (child_sum + parent_terms)
    return (
        first_inv.reshape(factor_one.shape),
        first_diag.reshape(diag_one.shape),
        second_inv.reshape(factor_two.shape),
        parent_inv.reshape(parent_block.shape),
        second_diag.reshape(diag_two.shape),
    )


def solution(mesh):
    placed = (
        P(None, "row", None, None, "col", None),
        P(None, "row", None, None, "col", None),
        P(None, "row", None, None, "col", None),
        P(None, "col", None, None),
        P(None, "col", None, None),
        P(None, "col", None, None),
        P(None, "row", None, "col"),
        P(None, "row", None, "col"),
        P(None, "col"),
    )
    return jax.shard_map(
        body,
        mesh=mesh,
        in_specs=placed,
        out_specs=(
            P(None, "row", None, None, "col", None),
            P(None, "col", None, None),
            P(None, "row", None, None, "col", None),
            P(None, "col", None, None),
            P(None, "col", None, None),
        ),
        check_vma=False,
    )
```

profile of v0, /device:TPU:40, one launch (start us, length us, event | category | flops | bytes accessed | tf_op | source)
XLA Modules:
  0.0 917.3 jit_solution(8874706373367763510)
XLA Ops:
  7.2 0.0 all-gather.4.cloned.1.call-start
  7.2 0.7 convert_bitcast_fusion
  8.0 1.7 copy_multiply_fusion
  9.7 0.0 all-gather.4.cloned.1.call-update
  9.7 0.0 all-gather.6.cloned.1.call-start
  9.8 1.8 copy.41
  11.6 0.0 all-gather.6.cloned.1.call-update
  11.6 0.0 all-gather.8.cloned.1.call-start
  12.3 1.6 bitcast_multiply_fusion
  13.9 0.0 all-reduce.6.cloned.1.call-start
  14.6 0.6 dynamic-slice.9
  15.2 138.5 %all-gather.4.cloned.1.call-done = bf16[1,32,256,2,1,256]{5,2,4,3,0,1:T(8,128)(2,1)} async-done(((bf16[1,1,256,2,1,256]{5,2,4,3,0,1:T(8,128)(2,1)}), bf16[1,32,256,2,1,256]{5,2,4,3,0,1:T(8,128)(2,1)}) %all-gather.4.cloned.1.call-update) | async-done | bytes 8388624 | tf_op jit(solution)/shard_map/all_gather | solution.py:44
  153.7 14.6 %copy.40 = bf16[1,32,256,2,1,256]{2,1,5,3,4,0:T(8,128)(2,1)} copy(bf16[1,32,256,2,1,256]{5,2,4,3,0,1:T(8,128)(2,1)} %all-gather.4.cloned.1.call-done) | data formatting | bytes 16777216 | tf_op jit(solution)/shard_map/all_gather | solution.py:44
  168.4 16.5 %copy.53 = bf16[64,8,32,256]{3,1,2,0:T(8,128)(2,1)} copy(bf16[64,8,32,256]{3,2,1,0:T(8,128)(2,1)} %bitcast.112) | data formatting | bytes 16777216
  184.8 12.1 %all-gather.6.cloned.1.call-done = bf16[1,1,256,2,16,256]{2,5,4,3,1,0:T(8,128)(2,1)} async-done(((bf16[1,1,256,2,1,256]{2,5,4,3,1,0:T(8,128)(2,1)}), bf16[1,1,256,2,16,256]{2,5,4,3,1,0:T(8,128)(2,1)}) %all-gather.6.cloned.1.call-update) | async-done | bytes 4194320 | tf_op jit(solution)/shard_map/all_gather | solution.py:39
  196.9 7.2 convolution_negate_fusion
  204.1 0.2 copy.43
  204.3 1.5 convolution_bitcast_fusion.1
  205.8 1.1 fusion.11
  207.0 0.0 all-reduce.4.cloned.1.call-start
  207.0 94.3 %all-gather.8.cloned.1.call-done = bf16[1,32,256,1,1,256]{5,2,4,3,0,1:T(8,128)(2,1)} async-done(((bf16[1,1,256,1,1,256]{5,2,4,3,0,1:T(8,128)(2,1)}), bf16[1,32,256,1,1,256]{5,2,4,3,0,1:T(8,128)(2,1)}) %all-gather.8.cloned.1.call-update) | async-done | bytes 4194320 | tf_op jit(solution)/shard_map/all_gather | solution.py:72
  301.3 4.8 convolution_bitcast_fusion.4
  306.1 0.2 copy.42
  306.4 0.9 fusion.9
  307.2 0.8 copy.49
  308.0 0.9 fusion.10
  308.9 0.9 multiply_convert_fusion.1
  309.9 309.2 %all-reduce.6.cloned.1.call-done = (f32[2,256,256]{2,1,0:T(8,128)}, f32[1,256,256]{2,1,0:T(8,128)}) async-done(((f32[2,256,256]{2,1,0:T(8,128)}, f32[1,256,256]{2,1,0:T(8,128)}), (f32[2,256,256]{2,1,0:T(8,128)}, f32[1,256,256]{2,1,0:T(8,128)})) %all-reduce.6.cloned.1.call-update) | async-done | bytes 786448 | tf_op jit(solution)/shard_map/psum | solution.py:61
  619.1 1.1 bitcast_subtract_fusion
  620.2 1.3 fusion.8
  621.6 287.4 %all-reduce.4.cloned.1.call-done = bf16[1,256,256]{2,1,0:T(8,128)(2,1)} async-done(((bf16[1,256,256]{2,1,0:T(8,128)(2,1)}), bf16[1,256,256]{2,1,0:T(8,128)(2,1)}) %all-reduce.4.cloned.1.call-update) | async-done | bytes 131088 | tf_op jit(solution)/shard_map/psum | solution.py:79
  909.0 1.8 fusion.7
  (17 shorter events, 0.1 us)
Async XLA Ops:
  7.2 299.2 %copy-start = (bf16[1,1,256,256]{3,2,1,0:T(8,128)(2,1)S(1)}, bf16[1,1,256,256]{3,2,1,0:T(8,128)(2,1)}, u32[]{:S(2)}) copy-start(bf16[1,1,256,256]{3,2,1,0:T(8,128)(2,1)} %param.12) | copy-start | bytes 393220
  7.2 146.6 %all-gather.4.cloned.1.call-start = ((), (), s32[]{:S(2)}) async-start(), calls=%async_computation | async-start | bytes 8650752 | tf_op jit(solution)/shard_map/all_gather | solution.py:44
  9.7 187.2 %all-gather.6.cloned.1.call-start = ((), (), s32[]{:S(2)}) async-start(), calls=%async_computation.1 | async-start | bytes 4456448 | tf_op jit(solution)/shard_map/all_gather | solution.py:39
  11.6 289.7 %all-gather.8.cloned.1.call-start = ((), (), s32[]{:S(2)}) async-start(), calls=%async_computation.2 | async-start | bytes 4325376 | tf_op jit(solution)/shard_map/all_gather | solution.py:72
  13.9 605.2 %all-reduce.6.cloned.1.call-start = ((), (), s32[]{:S(2)}) async-start(), calls=%async_computation.4 | async-start | bytes 1572864 | tf_op jit(solution)/shard_map/psum | solution.py:61
  196.9 7.4 copy-start.2
  196.9 8.9 copy-start.1
  207.0 702.0 %all-reduce.4.cloned.1.call-start = ((), (), s32[]{:S(2)}) async-start(), calls=%async_computation.3 | async-start | bytes 262144 | tf_op jit(solution)/shard_map/psum | solution.py:79
  301.3 317.8 %copy-start.4 = (f32[2,1,256,256]{3,2,1,0:T(8,128)S(1)}, f32[2,1,256,256]{3,2,1,0:T(8,128)}, u32[]{:S(2)}) copy-start(f32[2,1,256,256]{3,2,1,0:T(8,128)} %param.13) | copy-start | bytes 1572868
  306.1 602.9 %copy-start.6 = (f32[1,1,256,256]{3,2,1,0:T(8,128)S(1)}, f32[1,1,256,256]{3,2,1,0:T(8,128)}, u32[]{:S(2)}) copy-start(f32[1,1,256,256]{3,2,1,0:T(8,128)} %param.14) | copy-start | bytes 786436
  620.2 290.6 %copy-start.3 = (f32[2,256,256]{2,1,0:T(8,128)}, f32[2,256,256]{2,1,0:T(8,128)S(1)}, u32[]{:S(2)}) copy-start(f32[2,256,256]{2,1,0:T(8,128)S(1)} %bitcast_subtract_fusion) | copy-start | bytes 1572868
  621.5 289.3 %copy-start.5 = (bf16[1,256,256]{2,1,0:T(8,128)(2,1)}, bf16[1,256,256]{2,1,0:T(8,128)(2,1)S(1)}, u32[]{:S(2)}) copy-start(bf16[1,256,256]{2,1,0:T(8,128)(2,1)S(1)} %fusion.8) | copy-start | bytes 393220
Sparse Core Ops, SparseCore 0:
  11.8 141.9 all-gather.3
  156.4 40.4 all-gather.5
  200.7 100.6 all-gather.7
  304.7 314.3 all-reduce.5
  622.7 286.2 all-reduce.3
where the time goes:
time: 918 us; the launch traced here: 917 us
  waiting for transfers between devices  842 us (92%)
  local copies, waits for them, and re-layouts  34.7 us (4%)
  matrix products  19.5 us (2%)
  between operations  15.2 us (2%)
    psum x1, waiting for transfers between devices, body(): diag_sum, cross_sum = lax.psum((diag_part, cross_part), 'row')  309 us
    psum x1, waiting for transfers between devices, body(): lax.psum(child_part.astype(jnp.bfloat16), 'row').astype(jnp.float32)  287 us
    all_gather x1, waiting for transfers between devices, body(): lax.all_gather(first_factor, 'row', axis=1, tiled=True)  139 us
    all_gather x1, waiting for transfers between devices, body(): lax.all_gather(second_factor, 'row', axis=1, tiled=True)  94.3 us
    unnamed x17, local copies, waits for them, and re-layouts  19.1 us
  transfers between devices with their start and end apart: 5, of which 5 were waited for; matrix products, arithmetic and copies ran while one was open for 6% of the time, Pallas kernels for 0%

commit v1 on v0

--- a/solution.py
+++ b/solution.py
@@ -40,9 +40,11 @@
         anc_rows * block, anc_rows, grid_rows, block
     )
     add_rows = rows_step(whole_anc, anc_rows, block)
-    first_total = add_rows(
-        first_empty, lax.all_gather(first_factor, "row", axis=1, tiled=True), jnp.int32(0)
+    _solve_rates = lambda array_in, group_axis, d0: jnp.concatenate(
+        jax.lax.all_to_all(jnp.stack(jax.lax.axis_size(group_axis) * [array_in]), group_axis, 0, 0),
+        axis=d0,
     )
+    first_total = add_rows(first_empty, _solve_rates(first_factor, "row", 1), jnp.int32(0))
     first_shape = (anc_rows, block, first_count, block)
     second_shape = (anc_rows, block, second_count, block)
     first_keep = pattern_one.astype(jnp.float32)

time: 918 us -> 974 us (1.061)
  waiting for transfers between devices: 842 us -> 883 us
  starting transfers between devices: 0.21 us -> 16.2 us
    all_to_all x0 -> x1, waiting for transfers between devices: none -> 254 us  [body(): jax.lax.all_to_all(jnp.stack(jax.lax.axis_size(group_axis) * [array_in]),...]
    all_gather x1 -> x0, waiting for transfers between devices: 139 us -> none  [body(): lax.all_gather(first_factor, 'row', axis=1, tiled=True)]
    all_gather x1, waiting for transfers between devices: 94.3 us -> 32.2 us  [body(): lax.all_gather(second_factor, 'row', axis=1, tiled=True)]
    all_to_all x0 -> x1, starting transfers between devices: none -> 16 us  [body(): jax.lax.all_to_all(jnp.stack(jax.lax.axis_size(group_axis) * [array_in]),...]
    all_gather x1 -> x0, local copies, waits for them, and re-layouts: 14.6 us -> none  [body(): lax.all_gather(first_factor, 'row', axis=1, tiled=True)]
    all_gather x1, waiting for transfers between devices: 12.1 us -> 0.01 us  [body(): lax.all_gather(anc_inverse, 'col', axis=4, tiled=True)]
    all_to_all x0 -> x1, local copies, waits for them, and re-layouts: none -> 11.4 us  [body(): jax.lax.all_to_all(jnp.stack(jax.lax.axis_size(group_axis) * [array_in]),...]
  transfers between devices with their start and end apart: 5 -> 5, of which waited for: 5 -> 4; matrix products, arithmetic and copies ran while one was open for 6% -> 5% of each run, Pallas kernels for 0% -> 0%
where the time goes in v1:
time: 974 us
  waiting for transfers between devices  883 us (91%)
  local copies, waits for them, and re-layouts  35.2 us (4%)
  matrix products  19.3 us (2%)
  starting transfers between devices  16.2 us (2%)
  between operations  15.2 us (2%)
    psum x1, waiting for transfers between devices, body(): diag_sum, cross_sum = lax.psum((diag_part, cross_part), 'row')  310 us
    psum x1, waiting for transfers between devices, body(): lax.psum(child_part.astype(jnp.bfloat16), 'row').astype(jnp.float32)  287 us
    all_to_all x1, waiting for transfers between devices, body(): jax.lax.all_to_all(jnp.stack(jax.lax.axis_size(group_axis) * [array_in]),...  254 us
    all_gather x1, waiting for transfers between devices, body(): lax.all_gather(second_factor, 'row', axis=1, tiled=True)  32.2 us
  transfers between devices with their start and end apart: 5, of which 4 were waited for; matrix products, arithmetic and copies ran while one was open for 5% of the time, Pallas kernels for 0%

profile of v1, /device:TPU:40, one launch (start us, length us, event | category | flops | bytes accessed | tf_op | source)
XLA Modules:
  0.0 973.9 jit_solution(10576325178377848750)
XLA Ops:
  7.2 0.7 convert_bitcast_fusion
  7.9 1.2 multiply_bitcast_fusion
  9.2 0.2 copy.30
  9.3 4.3 stack.2
  13.6 16.0 %all-to-all-start = ((bf16[32,1,1,256,2,1,256]{3,6,4,5,2,1,0:T(8,128)(2,1)}), bf16[32,1,1,256,2,1,256]{3,6,4,5,2,1,0:T(8,128)(2,1)}, u32[]{:S(2)}, u32[]{:S(2)}) async-start(bf16[32,1,1,256,2,1,256]{3,6,4,5,2,1,0:T(8,128)(2,1)} %stack.2), calls=%async_computation | async-start | bytes 16777216 | tf_op jit(solution)/shard_map/all_to_all | solution.py:44
  29.6 0.0 all-gather.3.cloned.1.call-start
  29.7 0.9 copy.32
  30.6 0.0 all-gather.3.cloned.1.call-update
  30.6 0.0 all-gather.5.cloned.1.call-start
  31.3 0.7 bitcast_multiply_fusion
  32.0 0.0 all-reduce.6.cloned.1.call-start
  32.7 0.6 dynamic-slice.9
  33.3 254.5 %all-to-all-done = bf16[32,1,1,256,2,1,256]{3,6,4,5,2,1,0:T(8,128)(2,1)} async-done(((bf16[32,1,1,256,2,1,256]{3,6,4,5,2,1,0:T(8,128)(2,1)}), bf16[32,1,1,256,2,1,256]{3,6,4,5,2,1,0:T(8,128)(2,1)}, u32[]{:S(2)}, u32[]{:S(2)}) %all-to-all-start) | async-done | bytes 8388640 | tf_op jit(solution)/shard_map/all_to_all | solution.py:44
  287.8 11.4 %copy.31 = bf16[32,1,1,256,2,1,256]{3,0,6,4,5,2,1:T(8,128)(2,1)} copy(bf16[32,1,1,256,2,1,256]{3,6,4,5,2,1,0:T(8,128)(2,1)} %all-to-all-done) | data formatting | bytes 16777216 | tf_op jit(solution)/shard_map/all_to_all | solution.py:44
  299.2 16.6 %copy.43 = bf16[64,8,32,256]{3,1,2,0:T(8,128)(2,1)} copy(bf16[64,8,32,256]{3,2,1,0:T(8,128)(2,1)} %bitcast.112) | data formatting | bytes 16777216
  315.8 7.0 convolution_negate_fusion
  322.8 0.2 copy.34
  323.1 1.5 convolution_bitcast_fusion.1
  324.6 1.1 fusion.11
  325.7 0.0 all-reduce.4.cloned.1.call-start
  325.8 32.2 %all-gather.5.cloned.1.call-done = bf16[1,32,256,1,1,256]{5,2,4,3,0,1:T(8,128)(2,1)} async-done(((bf16[1,1,256,1,1,256]{5,2,4,3,0,1:T(8,128)(2,1)}), bf16[1,32,256,1,1,256]{5,2,4,3,0,1:T(8,128)(2,1)}) %all-gather.5.cloned.1.call-update) | async-done | bytes 4194320 | tf_op jit(solution)/shard_map/all_gather | solution.py:74
  357.9 4.8 convolution_bitcast_fusion.4
  362.7 0.2 copy.33
  363.0 0.9 fusion.9
  363.9 0.8 copy.40
  364.6 0.9 fusion.10
  365.5 0.9 multiply_convert_fusion.1
  366.5 309.7 %all-reduce.6.cloned.1.call-done = (f32[2,256,256]{2,1,0:T(8,128)}, f32[1,256,256]{2,1,0:T(8,128)}) async-done(((f32[2,256,256]{2,1,0:T(8,128)}, f32[1,256,256]{2,1,0:T(8,128)}), (f32[2,256,256]{2,1,0:T(8,128)}, f32[1,256,256]{2,1,0:T(8,128)})) %all-reduce.6.cloned.1.call-update) | async-done | bytes 786448 | tf_op jit(solution)/shard_map/psum | solution.py:63
  676.2 1.1 bitcast_subtract_fusion
  677.3 1.3 fusion.8
  678.6 286.8 %all-reduce.4.cloned.1.call-done = bf16[1,256,256]{2,1,0:T(8,128)(2,1)} async-done(((bf16[1,256,256]{2,1,0:T(8,128)(2,1)}), bf16[1,256,256]{2,1,0:T(8,128)(2,1)}) %all-reduce.4.cloned.1.call-update) | async-done | bytes 131088 | tf_op jit(solution)/shard_map/psum | solution.py:81
  965.5 1.8 fusion.7
  (20 shorter events, 0.1 us)
Async XLA Ops:
  7.2 355.8 %copy-start = (bf16[1,1,256,256]{3,2,1,0:T(8,128)(2,1)S(1)}, bf16[1,1,256,256]{3,2,1,0:T(8,128)(2,1)}, u32[]{:S(2)}) copy-start(bf16[1,1,256,256]{3,2,1,0:T(8,128)(2,1)} %param.12) | copy-start | bytes 393220
  13.6 16.1 %copy-start.6 = (bf16[1,1,256,2,1,256]{5,3,4,2,1,0:T(2,128)(2,1)S(1)}, bf16[1,1,256,2,1,256]{5,3,4,2,1,0:T(2,128)(2,1)}, u32[]{:S(2)}) copy-start(bf16[1,1,256,2,1,256]{5,3,4,2,1,0:T(2,128)(2,1)} %param.9) | copy-start | bytes 786436
  13.6 17.7 %copy-start.7 = (bf16[1,1,256,1,1,256]{5,2,4,3,1,0:T(8,128)(2,1)S(1)}, bf16[1,1,256,1,1,256]{5,2,4,3,1,0:T(8,128)(2,1)}, u32[]{:S(2)}) copy-start(bf16[1,1,256,1,1,256]{5,2,4,3,1,0:T(8,128)(2,1)} %param.11) | copy-start | bytes 393220
  13.6 274.2 %all-to-all-start = ((bf16[32,1,1,256,2,1,256]{3,6,4,5,2,1,0:T(8,128)(2,1)}), bf16[32,1,1,256,2,1,256]{3,6,4,5,2,1,0:T(8,128)(2,1)}, u32[]{:S(2)}, u32[]{:S(2)}) async-start(bf16[32,1,1,256,2,1,256]{3,6,4,5,2,1,0:T(8,128)(2,1)} %stack.2), calls=%async_computation | async-start | bytes 16777216 | tf_op jit(solution)/shard_map/all_to_all | solution.py:44
  29.6 286.2 %all-gather.3.cloned.1.call-start = ((), (), s32[]{:S(2)}) async-start(), calls=%async_computation.1 | async-start | bytes 4456448 | tf_op jit(solution)/shard_map/all_gather | solution.py:39
  30.6 327.3 %all-gather.5.cloned.1.call-start = ((), (), s32[]{:S(2)}) async-start(), calls=%async_computation.2 | async-start | bytes 4325376 | tf_op jit(solution)/shard_map/all_gather | solution.py:74
  32.0 644.1 %all-reduce.6.cloned.1.call-start = ((), (), s32[]{:S(2)}) async-start(), calls=%async_computation.4 | async-start | bytes 1572864 | tf_op jit(solution)/shard_map/psum | solution.py:63
  315.8 7.2 copy-start.1
  325.7 639.7 %all-reduce.4.cloned.1.call-start = ((), (), s32[]{:S(2)}) async-start(), calls=%async_computation.3 | async-start | bytes 262144 | tf_op jit(solution)/shard_map/psum | solution.py:81
  357.9 318.2 %copy-start.3 = (f32[2,1,256,256]{3,2,1,0:T(8,128)S(1)}, f32[2,1,256,256]{3,2,1,0:T(8,128)}, u32[]{:S(2)}) copy-start(f32[2,1,256,256]{3,2,1,0:T(8,128)} %param.13) | copy-start | bytes 1572868
  362.7 602.8 %copy-start.5 = (f32[1,1,256,256]{3,2,1,0:T(8,128)S(1)}, f32[1,1,256,256]{3,2,1,0:T(8,128)}, u32[]{:S(2)}) copy-start(f32[1,1,256,256]{3,2,1,0:T(8,128)} %param.14) | copy-start | bytes 786436
  677.3 290.1 %copy-start.2 = (f32[2,256,256]{2,1,0:T(8,128)}, f32[2,256,256]{2,1,0:T(8,128)S(1)}, u32[]{:S(2)}) copy-start(f32[2,256,256]{2,1,0:T(8,128)S(1)} %bitcast_subtract_fusion) | copy-start | bytes 1572868
  678.6 288.7 %copy-start.4 = (bf16[1,256,256]{2,1,0:T(8,128)(2,1)}, bf16[1,256,256]{2,1,0:T(8,128)(2,1)S(1)}, u32[]{:S(2)}) copy-start(bf16[1,256,256]{2,1,0:T(8,128)(2,1)S(1)} %fusion.8) | copy-start | bytes 393220
Sparse Core Ops, SparseCore 0:
  33.1 113.5 all-gather.2
  150.5 207.3 all-gather.4
  361.5 314.6 all-reduce.5
  679.2 286.2 all-reduce.3
